TPU v7x, 32 devices: a whole 2x2x4 slice. The times are simulated.
32 devices in a mesh: group: 2 (over y), ctx: 8 (over z, x), tp: 2 (over core).
Axes of the slice: x: 2, y: 2, z: 4, core: 2. Of those that a mesh axis runs over, the one named last changes fastest.
Arguments:
- hidden: bfloat16 [256, 16384], P(('group', 'ctx')), parts along dimension 0, may hold values from -6 to 6
- q_base: bfloat16 [256, 8192], P(('group', 'ctx'), 'tp'), parts along dimension 0, may hold values from -6 to 6
- adapter_down: bfloat16 [16, 16384, 64], P(('group', 'ctx')), parts along dimension 0, may hold values from -0.046875 to 0.046875
- adapter_up: bfloat16 [16, 64, 8192], P(('group', 'ctx'), None, 'tp'), parts along dimension 0, may hold values from -0.75 to 0.75
- adapter_owner: int32 [2], P('group'), parts along dimension 0, may hold values from 0 to 7
- turn_start: int32 [2], P('group'), parts along dimension 0, may hold values from 512 to 2047
- shard_lengths: int32 [16], P('group'), parts along dimension 0, may hold values from 1 to 64, 384 in all
- stored_keys: bfloat16 [1024, 512], P(('group', 'ctx'), 'tp'), parts along dimension 0, may hold values from -250 to 250
- stored_values: bfloat16 [1024, 512], P(('group', 'ctx'), 'tp'), parts along dimension 0, may hold values from -6 to 6
- unrotated_turn_keys: bfloat16 [256, 512], P(('group', 'ctx'), 'tp'), parts along dimension 0, may hold values from -15 to 15
- incoming_values: bfloat16 [256, 512], P(('group', 'ctx'), 'tp'), parts along dimension 0, may hold values from -6 to 6
Outputs:
- attended: bfloat16 [256, 8192], P(('group', 'ctx'), 'tp'), parts along dimension 0
There are 2 independent parts, one for each index of `group`. A program takes and returns all parts, laid end to end along the dimension named above; each array names one. Nothing has to cross between parts.
Inputs may be any that keep to these rules, and one draw needn't show every extreme that they name: The used slots of shard s are its slots 0 .. shard_lengths[s] - 1; some shard uses all 64.
All inputs are finite; a program needn't handle non-finite values.
Results may differ from a plain program's by a relative error of at most 0.019.
The roundings to bfloat16 on the way count: a program that leaves them out, or rounds other values in their place, can miss the bound.
Values may be sent and summed in bfloat16 or wider, within the bound.
No kernel may reach another device: no remote copies, remote signals or barrier semaphores. Data moves between devices by JAX's collectives and lax.ppermute only.
A program may use at most 64 MiB of HBM per device.

v0:
```python
import math
import jax
import jax.numpy as jnp
from jax import lax
from jax.sharding import PartitionSpec as P

HEAD_SIZE = 128


def spread(shard, axis, root):
    mine = lax.axis_index(axis) == root
    return lax.psum(jnp.where(mine, shard, jnp.zeros_like(shard)), axis)


def apply_rotary(values, token_positions, heads):
    half_dim = HEAD_SIZE // 2
    inverse = jnp.exp(
        jnp.arange(half_dim, dtype=jnp.float32) * (-2.0 * math.log(500000.0) / HEAD_SIZE)
    )
    angles = token_positions.astype(jnp.float32)[:, None] * inverse[None, :]
    cosine = jnp.cos(angles)[:, None, :]
    sine = jnp.sin(angles)[:, None, :]
    shaped = values.reshape(values.shape[0], heads, HEAD_SIZE)
    first = shaped[..., :half_dim]
    second = shaped[..., half_dim:]
    turned = jnp.concatenate(
        [first * cosine - second * sine, second * cosine + first * sine], axis=-1
    )
    return turned.reshape(values.shape[0], heads * HEAD_SIZE)


def shards(
    hidden,
    q_base,
    adapter_down,
    adapter_up,
    adapter_owner,
    turn_start,
    shard_lengths,
    stored_keys,
    stored_values,
    unrotated_turn_keys,
    incoming_values,
):
    holder = adapter_owner[0]
    slot_down = adapter_down[0]
    slot_up = adapter_up[0]
    got_down, got_up = (spread(slot_down, "ctx", holder), spread(slot_up, "ctx", holder))
    lowrank = jnp.dot(hidden, got_down, preferred_element_type=jnp.float32).astype(jnp.bfloat16)
    adapter_delta = jnp.dot(lowrank, got_up, preferred_element_type=jnp.float32)
    token_count = q_base.shape[0]
    slot_count = stored_keys.shape[0]
    shard_rows = token_count + slot_count
    ctx_size = lax.axis_size("ctx")
    myself = lax.axis_index("ctx")
    query_heads = q_base.shape[1] // HEAD_SIZE
    kv_heads = unrotated_turn_keys.shape[1] // HEAD_SIZE
    groups = query_heads // kv_heads
    local_tokens = jnp.arange(token_count, dtype=jnp.int32)
    token_positions = turn_start[0] + myself * token_count + local_tokens
    query_rows = apply_rotary(
        q_base.astype(jnp.float32) + 0.5 * adapter_delta, token_positions, query_heads
    ).astype(jnp.bfloat16)
    rotated_turn_keys = apply_rotary(
        unrotated_turn_keys.astype(jnp.float32), token_positions, kv_heads
    ).astype(jnp.bfloat16)
    grouped = query_rows.reshape(token_count, kv_heads, groups, HEAD_SIZE)
    key_here = jnp.concatenate([stored_keys, rotated_turn_keys], axis=0)
    value_here = jnp.concatenate([stored_values, incoming_values], axis=0)
    mine = myself * token_count + local_tokens
    score_scale = 1.0 / math.sqrt(HEAD_SIZE)
    shard_ids = jnp.arange(ctx_size, dtype=jnp.int32)

    def absorb(state, key_block, value_block, start):
        highest, denominator, accum = state
        row_count = key_block.shape[0]
        global_rows = start + jnp.arange(row_count, dtype=jnp.int32)
        owner_shard = global_rows // shard_rows
        within = global_rows % shard_rows
        is_cache = within < slot_count
        lengths_here = jnp.sum(
            jnp.where(owner_shard[:, None] == shard_ids[None, :], shard_lengths[None, :], 0), axis=1
        )
        token_number = owner_shard * token_count + (within - slot_count)
        allowed = jnp.where(
            is_cache[None, :],
            (within < lengths_here)[None, :],
            token_number[None, :] <= mine[:, None],
        )
        allowed = allowed[:, None, None, :]
        key_head_rows = key_block.reshape(-1, kv_heads, HEAD_SIZE)
        value_head_rows = value_block.reshape(-1, kv_heads, HEAD_SIZE)
        scores = (
            jnp.einsum("rhgd,khd->rhgk", grouped, key_head_rows, preferred_element_type=jnp.float32)
            * score_scale
        )
        new_high = jnp.maximum(highest, jnp.max(jnp.where(allowed, scores, -1e30), axis=-1))
        weights = jnp.where(allowed, jnp.exp(scores - new_high[..., None]), 0.0)
        fade = jnp.exp(highest - new_high)
        denominator = denominator * fade + jnp.sum(weights, axis=-1)
        product = jnp.einsum(
            "rhgk,khd->rhgd",
            weights.astype(jnp.bfloat16),
            value_head_rows,
            preferred_element_type=jnp.float32,
        )
        accum = accum * fade[..., None] + product
        return (new_high, denominator, accum)

    initial = (
        jnp.full((token_count, kv_heads, groups), -1e30, jnp.float32),
        jnp.zeros((token_count, kv_heads, groups), jnp.float32),
        jnp.zeros((token_count, kv_heads, groups, HEAD_SIZE), jnp.float32),
    )
    block_rows = shard_rows * 8

    def fold_pieces(state, pieces, start):
        key_piece, value_piece = pieces
        row_count = key_piece.shape[0]
        if row_count > block_rows and row_count % block_rows == 0:
            count = row_count // block_rows
            key_split = key_piece.reshape(count, block_rows, key_piece.shape[1])
            value_split = value_piece.reshape(count, block_rows, value_piece.shape[1])

            def inner(carry, items):
                key_one, value_one, number = items
                return (absorb(carry, key_one, value_one, start + number * block_rows), None)

            numbers = jnp.arange(count, dtype=jnp.int32)
            state, unused = lax.scan(inner, state, (key_split, value_split, numbers))
            return state
        return absorb(state, key_piece, value_piece, start)

    state = fold_pieces(
        initial,
        (
            lax.all_gather(key_here, "ctx", axis=0, tiled=True),
            lax.all_gather(value_here, "ctx", axis=0, tiled=True),
        ),
        jnp.int32(0),
    )
    highest, denominator, accum = state
    attended = accum / denominator[..., None]
    return attended.reshape(token_count, query_heads * HEAD_SIZE).astype(jnp.bfloat16)


def solution(mesh):
    return jax.shard_map(
        shards,
        mesh=mesh,
        in_specs=(
            P(("group", "ctx"), None),
            P(("group", "ctx"), "tp"),
            P(("group", "ctx"), None, None),
            P(("group", "ctx"), None, "tp"),
            P("group"),
            P("group"),
            P("group"),
            P(("group", "ctx"), "tp"),
            P(("group", "ctx"), "tp"),
            P(("group", "ctx"), "tp"),
            P(("group", "ctx"), "tp"),
        ),
        out_specs=P(("group", "ctx"), "tp"),
        check_vma=False,
    )
```

profile of v0, /device:TPU:0, one launch (start us, length us, event | category | flops | bytes accessed | tf_op | source)
XLA Modules:
  0.0 146.1 jit_solution(9558791827877660342)
XLA Ops:
  6.5 0.0 copy-start
  6.5 0.0 all-reduce.3.cloned.1.call-start
  7.3 0.0 copy-start.1
  7.3 3.1 %select_bitcast_fusion = bf16[16384,64]{0,1:T(8,128)(2,1)} fusion(bf16[1,16384,64]{1,2,0:T(8,128)(2,1)} %param.13, pred[]{:T(512)S(6)} %eq.22), kind=kLoop, calls=%fused_computation.2 | loop fusion | flops 1048576 | bytes 4194305 | tf_op jit(solution)/shard_map/jit(_where)/select_n | solution.py:12
  10.4 0.0 copy-done.1
  10.4 0.8 select_bitcast_fusion.1
  11.2 0.0 all-reduce.3.cloned.1.call-update
  11.2 0.0 copy-start.7
  11.3 0.0 copy-start.2
  12.0 0.0 copy-done.5
  12.0 0.1 multiply_cosine_fusion
  12.1 0.1 subtract_convert_fusion.1
  12.2 0.1 pad_maximum_fusion.3
  12.3 0.0 copy-done.3
  12.4 33.2 %all_gather.6 = bf16[640,256]{1,0:T(8,128)(2,1)S(1)} all-gather(bf16[80,256]{1,0:T(8,128)(2,1)S(1)} %pad_maximum_fusion.1), channel_id=1, replica_groups=mesh['group'=2,'ctx'=8,'tp'=2] {'ctx'}, dimensions={0}, use_global_device_ids=true | all-gather | bytes 368640 | tf_op jit(solution)/shard_map/all_gather | solution.py:137
  45.5 0.2 copy.39
  45.7 0.0 copy-done.4
  45.7 0.0 copy-done.6
  45.7 31.4 %all_gather.7 = bf16[640,256]{1,0:T(8,128)(2,1)S(1)} all-gather(bf16[80,256]{1,0:T(8,128)(2,1)S(1)} %pad_maximum_fusion.2), channel_id=1, replica_groups=mesh['group'=2,'ctx'=8,'tp'=2] {'ctx'}, dimensions={0}, use_global_device_ids=true | all-gather | bytes 368640 | tf_op jit(solution)/shard_map/all_gather | solution.py:138
  77.1 0.2 copy.42
  77.4 0.0 copy-done.7
  77.4 0.1 select_reduce_fusion.1
  77.5 0.1 compare_select_fusion
  77.6 56.6 %all-reduce.3.cloned.1.call-done = (bf16[64,4096]{1,0:T(8,128)(2,1)}, bf16[16384,64]{0,1:T(8,128)(2,1)}) async-done(((bf16[64,4096]{1,0:T(8,128)(2,1)}, bf16[16384,64]{0,1:T(8,128)(2,1)}), (bf16[64,4096]{1,0:T(8,128)(2,1)}, bf16[16384,64]{0,1:T(8,128)(2,1)})) %all-reduce.3.cloned.1.call-update) | async-done | bytes 2621456 | tf_op jit(solution)/shard_map/psum | solution.py:12
  134.2 2.6 %fusion.2 = f32[2,8,32,128]{3,1,2,0:T(8,128)S(1)} fusion(bf16[64,4096]{1,0:T(8,128)(2,1)} %get-tuple-element.5, bf16[16384,64]{0,1:T(8,128)(2,1)} %get-tuple-element.6, bf16[16,16384]{1,0:T(8,128)(2,1)S(1)} %copy-done, bf16[16,4096]{1,0:T(8,128)(2,1)S(1)} %copy-done.2), kind=kOutput, calls=%fused_computation.7 | convolution fusion | flops 42140672 | bytes 3538944 | tf_op jit(solution)/shard_map/dot_general | solution.py:50
  136.9 0.1 copy.52
  136.9 0.1 subtract_convert_fusion
  137.1 0.1 pad_maximum_fusion
  137.2 0.4 select_reduce_fusion
  137.6 0.4 fusion.6
  138.1 0.4 fusion.5
  138.5 0.7 copy.60
  (19 shorter events, 0.1 us)
Async XLA Ops:
  6.5 127.7 %copy-start = (bf16[16,16384]{1,0:T(8,128)(2,1)S(1)}, bf16[16,16384]{1,0:T(8,128)(2,1)}, u32[]{:S(2)}) copy-start(bf16[16,16384]{1,0:T(8,128)(2,1)} %param.11) | copy-start | bytes 1572868
  6.5 127.7 %all-reduce.3.cloned.1.call-start = ((), (), s32[]{:S(2)}) async-start(), calls=%async_computation | async-start | bytes 5242880 | tf_op jit(solution)/shard_map/psum | solution.py:12
  7.3 3.1 %copy-start.1 = (bf16[1,64,4096]{2,1,0:T(8,128)(2,1)S(1)}, bf16[1,64,4096]{2,1,0:T(8,128)(2,1)}, u32[]{:S(2)}) copy-start(bf16[1,64,4096]{2,1,0:T(8,128)(2,1)} %param.14) | copy-start | bytes 1572868
  11.2 0.8 copy-start.5
  11.2 1.1 copy-start.3
  11.2 34.5 %copy-start.4 = (bf16[64,256]{1,0:T(8,128)(2,1)S(1)}, bf16[64,256]{1,0:T(8,128)(2,1)}, u32[]{:S(2)}) copy-start(bf16[64,256]{1,0:T(8,128)(2,1)} %param.19) | copy-start | bytes 98308
  11.2 34.5 %copy-start.6 = (bf16[16,256]{1,0:T(8,128)(2,1)S(1)}, bf16[16,256]{1,0:T(8,128)(2,1)}, u32[]{:S(2)}) copy-start(bf16[16,256]{1,0:T(8,128)(2,1)} %param.21) | copy-start | bytes 24580
  11.2 66.2 %copy-start.7 = (s32[8]{0:T(128)S(1)}, s32[8]{0:T(128)}, u32[]{:S(2)}) copy-start(s32[8]{0:T(128)} %param.17) | copy-start | bytes 100
  11.3 123.0 %copy-start.2 = (bf16[16,4096]{1,0:T(8,128)(2,1)S(1)}, bf16[16,4096]{1,0:T(8,128)(2,1)}, u32[]{:S(2)}) copy-start(bf16[16,4096]{1,0:T(8,128)(2,1)} %param.12) | copy-start | bytes 393220
Sparse Core Ops, SparseCore 0:
  11.4 122.7 all-reduce.2
where the time goes:
time: 146 us
  blocking collectives  64.6 us (44%)
  waiting for transfers between devices  56.6 us (39%)
  between operations  15 us (10%)
  other arithmetic  5.13 us (4%)
  matrix products  3.5 us (2%)
    psum x1, waiting for transfers between devices, spread(): return lax.psum(jnp.where(mine, shard, jnp.zeros_like(shard)), axis)  56.6 us
    all_gather x1, blocking collectives, shards(): lax.all_gather(key_here, 'ctx', axis=0, tiled=True)  33.2 us
    all_gather x1, blocking collectives, shards(): lax.all_gather(value_here, 'ctx', axis=0, tiled=True)  31.4 us
    select_n x2, other arithmetic, spread(): return lax.psum(jnp.where(mine, shard, jnp.zeros_like(shard)), axis)  3.94 us
  transfers between devices with their start and end apart: 1, of which 1 were waited for; matrix products, arithmetic and copies ran while one was open for 1% of the time, Pallas kernels for 0%

commit v1 on v0

--- a/solution.py
+++ b/solution.py
@@ -7,9 +7,15 @@
 HEAD_SIZE = 128
 
 
+def summed_here(x, axis):
+    parts = lax.all_gather(x, axis, axis=0, tiled=False)
+    summed = parts.sum(axis=0)
+    return summed
+
+
 def spread(shard, axis, root):
     mine = lax.axis_index(axis) == root
-    return lax.psum(jnp.where(mine, shard, jnp.zeros_like(shard)), axis)
+    return summed_here(jnp.where(mine, shard, jnp.zeros_like(shard)), axis)
 
 
 def apply_rotary(values, token_positions, heads):

time: 146 us -> 341 us (2.34)
  waiting for transfers between devices: 56.6 us -> 236 us
  other arithmetic: 5.13 us -> 18.8 us
    all_gather x0 -> x2, waiting for transfers between devices: none -> 236 us  [summed_here(): parts = lax.all_gather(x, axis, axis=0, tiled=False)]
    psum x1 -> x0, waiting for transfers between devices: 56.6 us -> none  [spread(): return lax.psum(jnp.where(mine, shard, jnp.zeros_like(shard)), axis)]
    reduce_sum x0 -> x2, other arithmetic: none -> 12.1 us  [summed_here(): summed = parts.sum(axis=0)]
  transfers between devices with their start and end apart: 1 -> 2, of which waited for: 1 -> 2; matrix products, arithmetic and copies ran while one was open for 1% -> 3% of each run, Pallas kernels for 0% -> 0%
where the time goes in v1:
time: 341 us
  waiting for transfers between devices  236 us (69%)
  blocking collectives  65.1 us (19%)
  other arithmetic  18.8 us (6%)
  between operations  15 us (4%)
  local copies, waits for them, and re-layouts  3.8 us (1%)
    all_gather x2, waiting for transfers between devices, summed_here(): parts = lax.all_gather(x, axis, axis=0, tiled=False)  236 us
    all_gather x1, blocking collectives, shards(): lax.all_gather(value_here, 'ctx', axis=0, tiled=True)  32.7 us
    all_gather x1, blocking collectives, shards(): lax.all_gather(key_here, 'ctx', axis=0, tiled=True)  32.4 us
    reduce_sum x2, other arithmetic, summed_here(): summed = parts.sum(axis=0)  12.1 us
  transfers between devices with their start and end apart: 2, of which 2 were waited for; matrix products, arithmetic and copies ran while one was open for 3% of the time, Pallas kernels for 0%

profile of v1, /device:TPU:0, one launch (start us, length us, event | category | flops | bytes accessed | tf_op | source)
XLA Modules:
  0.0 340.7 jit_solution(7169124188076441398)
XLA Ops:
  7.3 1.9 broadcast_select_fusion.1
  9.1 0.0 all-gather.5.cloned.1.call-update
  9.2 0.0 all-gather.3.cloned.1.call-start
  9.2 3.1 broadcast_select_fusion
  12.3 0.0 all-gather.3.cloned.1.call-update
  12.3 0.0 copy-start.9
  13.1 0.1 multiply_cosine_fusion
  13.2 0.1 subtract_convert_fusion.1
  13.3 0.1 pad_maximum_fusion.3
  13.4 32.4 %all_gather.14 = bf16[640,256]{1,0:T(8,128)(2,1)S(1)} all-gather(bf16[80,256]{1,0:T(8,128)(2,1)S(1)} %pad_maximum_fusion.1), channel_id=1, replica_groups=mesh['group'=2,'ctx'=8,'tp'=2] {'ctx'}, dimensions={0}, use_global_device_ids=true | all-gather | bytes 368640 | tf_op jit(solution)/shard_map/all_gather | solution.py:143
  45.8 0.9 copy.39
  46.7 32.7 %all_gather.17 = bf16[640,256]{1,0:T(8,128)(2,1)S(1)} all-gather(bf16[80,256]{1,0:T(8,128)(2,1)S(1)} %pad_maximum_fusion.2), channel_id=1, replica_groups=mesh['group'=2,'ctx'=8,'tp'=2] {'ctx'}, dimensions={0}, use_global_device_ids=true | all-gather | bytes 368640 | tf_op jit(solution)/shard_map/all_gather | solution.py:144
  79.4 0.9 copy.42
  80.3 0.1 select_reduce_fusion.1
  80.4 0.7 compare_select_fusion
  81.1 10.4 %all-gather.5.cloned.1.call-done = bf16[8,64,4096]{2,1,0:T(8,128)(2,1)} async-done(((bf16[1,64,4096]{2,1,0:T(8,128)(2,1)}), bf16[8,64,4096]{2,1,0:T(8,128)(2,1)}) %all-gather.5.cloned.1.call-update) | async-done | bytes 4194320 | tf_op jit(solution)/shard_map/all_gather | solution.py:11
  91.5 2.9 reduce_sum.44
  94.4 0.0 copy-start.3
  94.4 225.7 %all-gather.3.cloned.1.call-done = bf16[8,16384,64]{1,2,0:T(8,128)(2,1)} async-done(((bf16[1,16384,64]{1,2,0:T(8,128)(2,1)}), bf16[8,16384,64]{1,2,0:T(8,128)(2,1)}) %all-gather.3.cloned.1.call-update) | async-done | bytes 16777232 | tf_op jit(solution)/shard_map/all_gather | solution.py:11
  320.2 9.1 %reduce_sum.43 = bf16[16384,64]{0,1:T(8,128)(2,1)S(1)} reduce(bf16[8,16384,64]{1,2,0:T(8,128)(2,1)} %all-gather.3.cloned.1.call-done, bf16[]{:T(256)} %constant.49.clone.1), dimensions={0}, to_apply=%region_1.2 | reduce | flops 7340032 | bytes 18874370 | tf_op jit(solution)/shard_map/reduce_sum | solution.py:12
  329.3 1.0 fusion.2
  330.3 0.0 copy-start.4
  330.3 0.1 copy.52
  330.4 0.1 subtract_convert_fusion
  330.5 0.1 pad_maximum_fusion
  330.7 0.6 copy-done.2
  331.3 0.0 copy-done.4
  331.3 0.4 select_reduce_fusion
  331.7 0.4 fusion.6
  332.2 0.5 copy-done.1
  332.7 0.4 fusion.5
  333.1 0.7 copy.60
  (28 shorter events, 0.1 us)
Async XLA Ops:
  6.5 322.8 %copy-start = (bf16[16,16384]{1,0:T(8,128)(2,1)S(1)}, bf16[16,16384]{1,0:T(8,128)(2,1)}, u32[]{:S(2)}) copy-start(bf16[16,16384]{1,0:T(8,128)(2,1)} %param.11) | copy-start | bytes 1572868
  6.5 85.0 %all-gather.5.cloned.1.call-start = ((), (), s32[]{:S(2)}) async-start(), calls=%async_computation.1 | async-start | bytes 4718592 | tf_op jit(solution)/shard_map/all_gather | solution.py:11
  9.2 311.0 %all-gather.3.cloned.1.call-start = ((), (), s32[]{:S(2)}) async-start(), calls=%async_computation | async-start | bytes 18874368 | tf_op jit(solution)/shard_map/all_gather | solution.py:11
  12.3 0.7 copy-start.7
  12.3 1.1 copy-start.5
  12.3 34.4 %copy-start.6 = (bf16[64,256]{1,0:T(8,128)(2,1)S(1)}, bf16[64,256]{1,0:T(8,128)(2,1)}, u32[]{:S(2)}) copy-start(bf16[64,256]{1,0:T(8,128)(2,1)} %param.19) | copy-start | bytes 98308
  12.3 34.4 %copy-start.8 = (bf16[16,256]{1,0:T(8,128)(2,1)S(1)}, bf16[16,256]{1,0:T(8,128)(2,1)}, u32[]{:S(2)}) copy-start(bf16[16,256]{1,0:T(8,128)(2,1)} %param.21) | copy-start | bytes 24580
  12.3 68.0 %copy-start.9 = (s32[8]{0:T(128)S(1)}, s32[8]{0:T(128)}, u32[]{:S(2)}) copy-start(s32[8]{0:T(128)} %param.17) | copy-start | bytes 100
  94.4 234.9 %copy-start.3 = (bf16[16,4096]{1,0:T(8,128)(2,1)S(1)}, bf16[16,4096]{1,0:T(8,128)(2,1)}, u32[]{:S(2)}) copy-start(bf16[16,4096]{1,0:T(8,128)(2,1)} %param.12) | copy-start | bytes 393220
  330.3 1.0 copy-start.2
  330.3 1.0 copy-start.4
  331.7 1.0 copy-start.1
Sparse Core Ops, SparseCore 0:
  9.5 81.9 all-gather.4
  93.6 226.5 all-gather.2
